TPU v7x, 512 devices: a whole 4x8x8 slice. The times are simulated.
512 devices in a mesh: dp: 64 (over z_hi, x, y), tile: 8 (over z_lo, core).
Axes of the slice: x: 4, y: 8, z: 8 (z_hi: 2, z_lo: 4; z = z_hi * 4 + z_lo), core: 2. Of those that a mesh axis runs over, the one named last changes fastest.
Arguments:
- feats: bfloat16 [4096, 2048], P('dp'), may hold values from -11 to 11
- jitter: bfloat16 [4096, 2048], P('dp'), may hold values from -1.5 to 1.5
- mask_ids: int32 [4096, 2], P('dp'), may hold values from 0 to 31
- proj_weight: bfloat16 [2048, 4096], P('dp', 'tile'), may hold values from -0.125 to 0.125
Outputs:
- feats_grad: float32 [4096, 2048], P('dp', 'tile')
- diag_corr: float32 [4096], P('tile')
- cross_power: float32 [], replicated
All inputs are finite; a program needn't handle non-finite values.
Results may differ from a plain program's by a relative error of at most 0.02.
Values may be sent and summed in bfloat16 or wider, within the bound.
No kernel may reach another device: no remote copies, remote signals or barrier semaphores. Data moves between devices by JAX's collectives and lax.ppermute only.
A program may use at most 64 MiB of HBM per device.

v0:
```python
import jax
import jax.numpy as jnp
from jax import lax
from jax.sharding import PartitionSpec as P

EMB = 4096
GROUPS = 32
LAMBDA_OFF = 0.0051
NORM_EPS = 1e-05
LOSS_SCALE = 65536.0


def masked_views(feats, jitter, mask_ids):
    width = feats.shape[1]
    group_size = width // GROUPS
    channel_group = lax.broadcasted_iota(jnp.int32, (1, width), 1) // group_size
    keep_a = (channel_group != mask_ids[:, 0:1]).astype(jnp.float32)
    keep_b = (channel_group != mask_ids[:, 1:2]).astype(jnp.float32)
    values = feats.astype(jnp.float32)
    view_a = (values * keep_a).astype(jnp.bfloat16)
    view_b = (values * keep_b + jitter.astype(jnp.float32)).astype(jnp.bfloat16)
    return (view_a, view_b, keep_a, keep_b)


def contract_last(left, right):
    return lax.dot_general(
        left, right, (((1,), (1,)), ((), ())), preferred_element_type=jnp.float32
    )


def on_device(feats, jitter, mask_ids, proj_weight):
    view_a, view_b, keep_a, keep_b = masked_views(feats, jitter, mask_ids)
    rows = feats.shape[0]
    total = rows * lax.axis_size("dp")
    piece = lax.all_gather(proj_weight, "dp", axis=0, tiled=True)
    raw_a = jnp.dot(view_a, piece, preferred_element_type=jnp.float32)
    raw_b = jnp.dot(view_b, piece, preferred_element_type=jnp.float32)
    raw_a = raw_a.astype(jnp.bfloat16)
    raw_b = raw_b.astype(jnp.bfloat16)
    values_a = raw_a.astype(jnp.float32)
    values_b = raw_b.astype(jnp.float32)
    moment_sums = lax.psum(
        (
            jnp.sum(values_a, axis=0),
            jnp.sum(values_a * values_a, axis=0),
            jnp.sum(values_b, axis=0),
            jnp.sum(values_b * values_b, axis=0),
        ),
        "dp",
    )
    mean_a = moment_sums[0] / total
    mean_b = moment_sums[2] / total
    inv_a = lax.rsqrt(moment_sums[1] / total - mean_a * mean_a + NORM_EPS)
    inv_b = lax.rsqrt(moment_sums[3] / total - mean_b * mean_b + NORM_EPS)
    norm_a = ((values_a - mean_a) * inv_a).astype(jnp.bfloat16)
    norm_b = ((values_b - mean_b) * inv_b).astype(jnp.bfloat16)
    outgoing_a, outgoing_b = (norm_a, norm_b)
    gathered_a, gathered_b = (
        lax.all_gather(outgoing_a, "dp", axis=0, tiled=True),
        lax.all_gather(outgoing_b, "dp", axis=0, tiled=True),
    )
    whole_a, whole_b = (gathered_a, gathered_b)
    za = norm_a.astype(jnp.float32)
    zb = norm_b.astype(jnp.float32)
    diag_corr = jnp.sum(whole_a.astype(jnp.float32) * whole_b.astype(jnp.float32), axis=0) / total
    gram_a, gram_b = (
        lax.psum(contract_last(norm_a, whole_a).astype(jnp.bfloat16), "tile").astype(jnp.float32),
        lax.psum(contract_last(norm_b, whole_b).astype(jnp.bfloat16), "tile").astype(jnp.float32),
    )
    trace_part = jnp.sum(gram_a * gram_b)
    gram_bf_a = gram_a.astype(jnp.bfloat16)
    gram_bf_b = gram_b.astype(jnp.bfloat16)
    coeff = -2.0 * (1.0 - diag_corr) - 2.0 * LAMBDA_OFF * diag_corr
    factor = 2.0 * LAMBDA_OFF / (total * total)
    grad_na = zb * coeff / total + factor * jnp.dot(
        gram_bf_b, whole_a, preferred_element_type=jnp.float32
    )
    grad_nb = za * coeff / total + factor * jnp.dot(
        gram_bf_a, whole_b, preferred_element_type=jnp.float32
    )
    sums = lax.psum(
        (
            jnp.sum(grad_na, axis=0),
            jnp.sum(grad_na * za, axis=0),
            jnp.sum(grad_nb, axis=0),
            jnp.sum(grad_nb * zb, axis=0),
            trace_part,
        ),
        "dp",
    )
    dz_a = (inv_a * (grad_na - sums[0] / total - za * (sums[1] / total))).astype(jnp.bfloat16)
    dz_b = (inv_b * (grad_nb - sums[2] / total - zb * (sums[3] / total))).astype(jnp.bfloat16)
    cross_power = sums[4] / (total * total) / EMB
    piece = lax.all_gather(proj_weight, "dp", axis=0, tiled=True)
    combined = keep_a * contract_last(dz_a, piece) + keep_b * contract_last(dz_b, piece)
    feats_grad = LOSS_SCALE * lax.psum_scatter(
        combined.astype(jnp.bfloat16), "tile", scatter_dimension=1, tiled=True
    ).astype(jnp.float32)
    return (feats_grad, diag_corr, cross_power)


def solution(mesh):
    in_specs = (P("dp", None), P("dp", None), P("dp", None), P("dp", "tile"))
    out_specs = (P("dp", "tile"), P("tile"), P())
    return jax.shard_map(
        on_device, mesh=mesh, in_specs=in_specs, out_specs=out_specs, check_vma=False
    )
```

profile of v0, /device:TPU:2, one launch (start us, length us, event | category | flops | bytes accessed | tf_op | source)
XLA Modules:
  0.0 1044.2 jit_solution(3339325027411994053)
XLA Ops:
  7.2 0.0 all-gather.4.cloned.1.call-start
  7.2 0.7 all-gather.4.cloned.1.call-update
  7.9 0.0 all-gather.6.cloned.1.call-start
  8.0 0.8 slice_bitcast_fusion
  8.7 147.5 %all-gather.4.cloned.1.call-done = bf16[2048,512]{1,0:T(8,128)(2,1)} async-done(((bf16[32,512]{1,0:T(8,128)(2,1)}), bf16[2048,512]{1,0:T(8,128)(2,1)}) %all-gather.4.cloned.1.call-update) | async-done | bytes 2097168 | tf_op jit(solution)/shard_map/all_gather | solution.py:35
  156.2 2.2 multiply_reduce_fusion.3
  158.5 2.3 fusion.42
  160.8 186.2 %all-reduce.1 = (f32[512]{0:T(512)S(1)}, f32[512]{0:T(512)S(1)}, f32[512]{0:T(512)S(1)}, f32[512]{0:T(512)S(1)}) all-reduce(f32[512]{0:T(512)S(1)} %get-tuple-element.10, f32[512]{0:T(512)S(1)} %get-tuple-element.9, f32[512]{0:T(512)S(1)} %get-tuple-element.8, f32[512]{0:T(512)S(1)} %get-tuple-element.7), channel_id=1, replica_groups=mesh['dp'=64,'tile'=8] {'dp'}, use_global_device_ids=true, to_apply=%region_3.4 | all-reduce | flops 2048 | bytes 16384 | tf_op jit(solution)/shard_map/psum | solution.py:42
  347.0 0.6 multiply_convert_fusion
  347.6 0.0 all-gather.6.cloned.1.call-update
  347.6 0.0 all-gather.8.cloned.1.call-start
  347.7 0.6 multiply_convert_fusion.1
  348.3 0.0 copy-start.3
  348.3 0.0 all-gather.8.cloned.1.call-update
  348.4 0.0 all-reduce.5.cloned.1.call-start
  348.4 186.0 %all-gather.6.cloned.1.call-done = bf16[4096,512]{1,0:T(8,128)(2,1)} async-done(((bf16[64,512]{1,0:T(8,128)(2,1)}), bf16[4096,512]{1,0:T(8,128)(2,1)}) %all-gather.6.cloned.1.call-update) | async-done | bytes 4194320 | tf_op jit(solution)/shard_map/all_gather | solution.py:59
  534.4 4.4 convolution_convert_fusion
  538.8 152.4 %all-gather.8.cloned.1.call-done = bf16[4096,512]{1,0:T(8,128)(2,1)} async-done(((bf16[64,512]{1,0:T(8,128)(2,1)}), bf16[4096,512]{1,0:T(8,128)(2,1)}) %all-gather.8.cloned.1.call-update) | async-done | bytes 4194320 | tf_op jit(solution)/shard_map/all_gather | solution.py:60
  691.2 0.0 copy-done.3
  691.2 4.4 convolution_convert_fusion.1
  695.6 0.0 all-reduce.5.cloned.1.call-update
  695.6 0.0 copy-start.2
  695.6 0.0 reduce-scatter.2.cloned.1.call-start
  695.6 4.6 multiply_reduce_fusion
  700.3 0.6 multiply_subtract_fusion
  700.8 68.8 %all-reduce.5.cloned.1.call-done = (bf16[64,4096]{1,0:T(8,128)(2,1)}, bf16[64,4096]{1,0:T(8,128)(2,1)}) async-done(((bf16[64,4096]{1,0:T(8,128)(2,1)}, bf16[64,4096]{1,0:T(8,128)(2,1)}), (bf16[64,4096]{1,0:T(8,128)(2,1)}, bf16[64,4096]{1,0:T(8,128)(2,1)})) %all-reduce.5.cloned.1.call-update) | async-done | bytes 1048592 | tf_op jit(solution)/shard_map/psum | solution.py:68
  769.7 0.0 copy-start
  769.7 0.0 copy-start.4
  769.7 2.2 multiply_reduce_fusion.1
  771.9 0.0 copy-done.2
  771.9 0.0 copy-start.1
  771.9 3.4 fusion.40
  775.3 0.0 copy-done
  775.3 0.0 copy-done.4
  775.3 0.9 fusion.41
  776.2 196.4 %all-reduce = (f32[512]{0:T(512)S(1)}, f32[512]{0:T(512)S(1)}, f32[512]{0:T(512)S(1)}, f32[512]{0:T(512)S(1)}, f32[]{:T(128)}) all-reduce(f32[512]{0:T(512)S(1)} %get-tuple-element.6, f32[512]{0:T(512)S(1)} %get-tuple-element.5, f32[512]{0:T(512)S(1)} %get-tuple-element.4, ...), channel_id=1, replica_groups=mesh['dp'=64,'tile'=8] {'dp'}, use_global_device_ids=true, to_apply=%region_13.14 | all-reduce | flops 2049 | bytes 16392 | tf_op jit(solution)/shard_map/psum | solution.py:81
  972.6 0.0 copy-done.1
  972.6 0.8 convolution_select_fusion.1
  973.3 1.5 fusion.1
  974.8 0.0 reduce-scatter.2.cloned.1.call-update
  975.4 59.7 %reduce-scatter.2.cloned.1.call-done = bf16[64,256]{1,0:T(8,128)(2,1)} async-done(((bf16[64,2048]{1,0:T(8,128)(2,1)}), bf16[64,256]{1,0:T(8,128)(2,1)}) %reduce-scatter.2.cloned.1.call-update) | async-done | bytes 32784 | tf_op jit(solution)/shard_map/reduce_scatter | solution.py:96
  1035.1 1.4 convert_multiply_fusion.6
  (5 shorter events, 0.0 us)
Async XLA Ops:
  7.2 149.1 %all-gather.4.cloned.1.call-start = ((), (), s32[]{:S(2)}) async-start(), calls=%async_computation.1 | async-start | bytes 2129920 | tf_op jit(solution)/shard_map/all_gather | solution.py:35
  7.9 526.5 %all-gather.6.cloned.1.call-start = ((), (), s32[]{:S(2)}) async-start(), calls=%async_computation.2 | async-start | bytes 4259840 | tf_op jit(solution)/shard_map/all_gather | solution.py:59
  347.6 343.6 %all-gather.8.cloned.1.call-start = ((), (), s32[]{:S(2)}) async-start(), calls=%async_computation.3 | async-start | bytes 4259840 | tf_op jit(solution)/shard_map/all_gather | solution.py:60
  348.3 342.9 %copy-start.3 = (bf16[64,512]{1,0:T(8,128)(2,1)S(1)}, bf16[64,512]{1,0:T(8,128)(2,1)}, u32[]{:S(2)}) copy-start(bf16[64,512]{1,0:T(8,128)(2,1)} %multiply_convert_fusion.1) | copy-start | bytes 196612
  348.4 421.3 %all-reduce.5.cloned.1.call-start = ((), (), s32[]{:S(2)}) async-start(), calls=%async_computation.5 | async-start | bytes 2097152 | tf_op jit(solution)/shard_map/psum | solution.py:68
  695.6 76.3 %copy-start.2 = (bf16[64,512]{1,0:T(8,128)(2,1)S(1)}, bf16[64,512]{1,0:T(8,128)(2,1)}, u32[]{:S(2)}) copy-start(bf16[64,512]{1,0:T(8,128)(2,1)} %multiply_convert_fusion) | copy-start | bytes 196612
  695.6 339.5 %reduce-scatter.2.cloned.1.call-start = ((), (), s32[]{:S(2)}) async-start(), calls=%async_computation.4 | async-start | bytes 294912 | tf_op jit(solution)/shard_map/reduce_scatter | solution.py:96
  769.7 5.6 copy-start
  769.7 5.6 copy-start.4
  771.9 200.6 %copy-start.1 = (bf16[2048,512]{1,0:T(8,128)(2,1)S(1)}, bf16[2048,512]{1,0:T(8,128)(2,1)}, u32[]{:S(2)}) copy-start(bf16[2048,512]{1,0:T(8,128)(2,1)} %all-gather.4.cloned.1.call-done) | copy-start | bytes 6291460
Sparse Core Ops, SparseCore 0:
  12.5 143.6 all-gather.3
  347.7 186.5 all-gather.5
  538.9 152.2 all-gather.7
  695.7 73.9 all-reduce.4
  974.9 60.1 reduce-scatter.1
where the time goes:
time: 1040 us
  waiting for transfers between devices  615 us (59%)
  blocking collectives  383 us (37%)
  matrix products  19.7 us (2%)
  between operations  15.6 us (2%)
    psum x1, blocking collectives, on_device(): lax.psum((jnp.sum(grad_na, axis=0), jnp.sum(grad_na * za, axis=0), jnp.su...  196 us
    psum x1, blocking collectives, on_device(): lax.psum((jnp.sum(values_a, axis=0), jnp.sum(values_a * values_a, axis=0)...  186 us
    all_gather x1, waiting for transfers between devices, on_device(): lax.all_gather(outgoing_a, 'dp', axis=0, tiled=True)  186 us
    all_gather x1, waiting for transfers between devices, on_device(): lax.all_gather(outgoing_b, 'dp', axis=0, tiled=True)  152 us
    all_gather x1, waiting for transfers between devices, on_device(): piece = lax.all_gather(proj_weight, 'dp', axis=0, tiled=True)  148 us
    psum x1, waiting for transfers between devices, on_device(): lax.psum(contract_last(norm_b, whole_b).astype(jnp.bfloat16), 'tile')  68.8 us
    reduce_scatter x1, waiting for transfers between devices, on_device(): lax.psum_scatter(combined.astype(jnp.bfloat16), 'tile', scatter_dimension...  59.7 us
  transfers between devices with their start and end apart: 5, of which 5 were waited for; matrix products, arithmetic and copies ran while one was open for 1% of the time, Pallas kernels for 0%

commit v1 on v0

--- a/solution.py
+++ b/solution.py
@@ -56,7 +56,10 @@
     norm_b = ((values_b - mean_b) * inv_b).astype(jnp.bfloat16)
     outgoing_a, outgoing_b = (norm_a, norm_b)
     gathered_a, gathered_b = (
-        lax.all_gather(outgoing_a, "dp", axis=0, tiled=True),
+        jnp.concatenate(
+            lax.all_to_all(jnp.stack([outgoing_a for _ in range(lax.axis_size("dp"))]), "dp", 0, 0),
+            axis=0,
+        ),
         lax.all_gather(outgoing_b, "dp", axis=0, tiled=True),
     )
     whole_a, whole_b = (gathered_a, gathered_b)

time: 1040 us -> 950 us (0.913)
  the two profiles are of different devices: /device:TPU:2 before, /device:TPU:4 now
where the time goes in v1:
time: 950 us; the launch traced here: 949 us
  waiting for transfers between devices  498 us (52%)
  blocking collectives  323 us (34%)
  starting transfers between devices  80.3 us (8%)
  matrix products  19.7 us (2%)
  between operations  15.6 us (2%)
  other arithmetic  9.51 us (1%)
    psum x1, blocking collectives, on_device(): lax.psum((jnp.sum(grad_na, axis=0), jnp.sum(grad_na * za, axis=0), jnp.su...  165 us
    psum x1, blocking collectives, on_device(): lax.psum((jnp.sum(values_a, axis=0), jnp.sum(values_a * values_a, axis=0)...  158 us
    all_gather x1, waiting for transfers between devices, on_device(): piece = lax.all_gather(proj_weight, 'dp', axis=0, tiled=True)  148 us
    all_gather x1, waiting for transfers between devices, on_device(): lax.all_gather(outgoing_b, 'dp', axis=0, tiled=True)  128 us
    reduce_scatter x1, waiting for transfers between devices, on_device(): lax.psum_scatter(combined.astype(jnp.bfloat16), 'tile', scatter_dimension...  91 us
    all_to_all x1, starting transfers between devices, on_device(): lax.all_to_all(jnp.stack([outgoing_a for _ in range(lax.axis_size('dp'))]...  80.2 us
    psum x1, waiting for transfers between devices, on_device(): lax.psum(contract_last(norm_b, whole_b).astype(jnp.bfloat16), 'tile')  68.8 us
    all_to_all x1, waiting for transfers between devices, on_device(): lax.all_to_all(jnp.stack([outgoing_a for _ in range(lax.axis_size('dp'))]...  61.5 us
  transfers between devices with their start and end apart: 5, of which 5 were waited for; matrix products, arithmetic and copies ran while one was open for 1% of the time, Pallas kernels for 0%

profile of v1, /device:TPU:4, one launch (start us, length us, event | category | flops | bytes accessed | tf_op | source)
XLA Modules:
  0.0 949.3 jit_solution(12050009236728042560)
XLA Ops:
  7.2 0.0 all-gather.3.cloned.1.call-start
  7.2 0.7 all-gather.3.cloned.1.call-update
  7.9 0.8 slice_bitcast_fusion
  8.7 147.6 %all-gather.3.cloned.1.call-done = bf16[2048,512]{1,0:T(8,128)(2,1)} async-done(((bf16[32,512]{1,0:T(8,128)(2,1)}), bf16[2048,512]{1,0:T(8,128)(2,1)}) %all-gather.3.cloned.1.call-update) | async-done | bytes 2097168 | tf_op jit(solution)/shard_map/all_gather | solution.py:35
  156.3 2.2 multiply_reduce_fusion.3
  158.5 2.3 fusion.42
  160.8 157.7 %all-reduce.1 = (f32[512]{0:T(512)S(1)}, f32[512]{0:T(512)S(1)}, f32[512]{0:T(512)S(1)}, f32[512]{0:T(512)S(1)}) all-reduce(f32[512]{0:T(512)S(1)} %get-tuple-element.10, f32[512]{0:T(512)S(1)} %get-tuple-element.9, f32[512]{0:T(512)S(1)} %get-tuple-element.8, f32[512]{0:T(512)S(1)} %get-tuple-element.7), channel_id=1, replica_groups=mesh['dp'=64,'tile'=8] {'dp'}, use_global_device_ids=true, to_apply=%region_3.4 | all-reduce | flops 2048 | bytes 16384 | tf_op jit(solution)/shard_map/psum | solution.py:42
  318.6 2.5 stack.2
  321.0 80.2 %all-to-all-start = ((bf16[64,64,512]{2,1,0:T(8,128)(2,1)}), bf16[64,64,512]{2,1,0:T(8,128)(2,1)}, u32[]{:S(2)}, u32[]{:S(2)}) async-start(bf16[64,64,512]{2,1,0:T(8,128)(2,1)} %stack.2), calls=%async_computation | async-start | bytes 8388608 | tf_op jit(solution)/shard_map/all_to_all | solution.py:60
  401.2 0.0 all-gather.5.cloned.1.call-start
  401.3 0.6 multiply_convert_fusion.1
  401.9 0.0 copy-start.2
  401.9 0.0 all-gather.5.cloned.1.call-update
  402.0 0.0 all-reduce.5.cloned.1.call-start
  402.0 61.5 %all-to-all-done = bf16[64,64,512]{2,1,0:T(8,128)(2,1)} async-done(((bf16[64,64,512]{2,1,0:T(8,128)(2,1)}), bf16[64,64,512]{2,1,0:T(8,128)(2,1)}, u32[]{:S(2)}, u32[]{:S(2)}) %all-to-all-start) | async-done | bytes 4194336 | tf_op jit(solution)/shard_map/all_to_all | solution.py:60
  463.5 4.4 convolution_convert_fusion
  467.8 128.5 %all-gather.5.cloned.1.call-done = bf16[4096,512]{1,0:T(8,128)(2,1)} async-done(((bf16[64,512]{1,0:T(8,128)(2,1)}), bf16[4096,512]{1,0:T(8,128)(2,1)}) %all-gather.5.cloned.1.call-update) | async-done | bytes 4194320 | tf_op jit(solution)/shard_map/all_gather | solution.py:63
  596.3 0.0 copy-done.2
  596.3 4.4 convolution_convert_fusion.1
  600.7 0.0 all-reduce.5.cloned.1.call-update
  600.7 0.0 reduce-scatter.2.cloned.1.call-start
  600.7 4.6 multiply_reduce_fusion
  605.3 0.6 multiply_subtract_fusion
  605.9 68.8 %all-reduce.5.cloned.1.call-done = (bf16[64,4096]{1,0:T(8,128)(2,1)}, bf16[64,4096]{1,0:T(8,128)(2,1)}) async-done(((bf16[64,4096]{1,0:T(8,128)(2,1)}, bf16[64,4096]{1,0:T(8,128)(2,1)}), (bf16[64,4096]{1,0:T(8,128)(2,1)}, bf16[64,4096]{1,0:T(8,128)(2,1)})) %all-reduce.5.cloned.1.call-update) | async-done | bytes 1048592 | tf_op jit(solution)/shard_map/psum | solution.py:71
  674.7 0.0 copy-start
  674.7 0.0 copy-start.3
  674.7 2.2 multiply_reduce_fusion.1
  677.0 0.0 copy-start.1
  677.0 3.4 fusion.41
  680.3 0.0 copy-done
  680.3 0.0 copy-done.3
  680.4 0.9 fusion.40
  681.2 165.1 %all-reduce = (f32[512]{0:T(512)S(1)}, f32[512]{0:T(512)S(1)}, f32[512]{0:T(512)S(1)}, f32[512]{0:T(512)S(1)}, f32[]{:T(128)}) all-reduce(f32[512]{0:T(512)S(1)} %get-tuple-element.6, f32[512]{0:T(512)S(1)} %get-tuple-element.5, f32[512]{0:T(512)S(1)} %get-tuple-element.4, ...), channel_id=1, replica_groups=mesh['dp'=64,'tile'=8] {'dp'}, use_global_device_ids=true, to_apply=%region_13.14 | all-reduce | flops 2049 | bytes 16392 | tf_op jit(solution)/shard_map/psum | solution.py:84
  846.3 0.0 copy-done.1
  846.3 0.8 convolution_select_fusion.1
  847.1 1.5 fusion.1
  848.5 0.0 reduce-scatter.2.cloned.1.call-update
  849.2 91.0 %reduce-scatter.2.cloned.1.call-done = bf16[64,256]{1,0:T(8,128)(2,1)} async-done(((bf16[64,2048]{1,0:T(8,128)(2,1)}), bf16[64,256]{1,0:T(8,128)(2,1)}) %reduce-scatter.2.cloned.1.call-update) | async-done | bytes 32784 | tf_op jit(solution)/shard_map/reduce_scatter | solution.py:99
  940.2 1.4 convert_multiply_fusion.6
  (7 shorter events, 0.0 us)
Async XLA Ops:
  7.2 149.1 %all-gather.3.cloned.1.call-start = ((), (), s32[]{:S(2)}) async-start(), calls=%async_computation.2 | async-start | bytes 2129920 | tf_op jit(solution)/shard_map/all_gather | solution.py:35
  321.0 142.4 %all-to-all-start = ((bf16[64,64,512]{2,1,0:T(8,128)(2,1)}), bf16[64,64,512]{2,1,0:T(8,128)(2,1)}, u32[]{:S(2)}, u32[]{:S(2)}) async-start(bf16[64,64,512]{2,1,0:T(8,128)(2,1)} %stack.2), calls=%async_computation | async-start | bytes 8388608 | tf_op jit(solution)/shard_map/all_to_all | solution.py:60
  401.2 195.1 %all-gather.5.cloned.1.call-start = ((), (), s32[]{:S(2)}) async-start(), calls=%async_computation.3 | async-start | bytes 4259840 | tf_op jit(solution)/shard_map/all_gather | solution.py:63
  401.9 194.4 %copy-start.2 = (bf16[64,512]{1,0:T(8,128)(2,1)S(1)}, bf16[64,512]{1,0:T(8,128)(2,1)}, u32[]{:S(2)}) copy-start(bf16[64,512]{1,0:T(8,128)(2,1)} %multiply_convert_fusion.1) | copy-start | bytes 196612
  402.0 272.8 %all-reduce.5.cloned.1.call-start = ((), (), s32[]{:S(2)}) async-start(), calls=%async_computation.5 | async-start | bytes 2097152 | tf_op jit(solution)/shard_map/psum | solution.py:71
  600.7 339.5 %reduce-scatter.2.cloned.1.call-start = ((), (), s32[]{:S(2)}) async-start(), calls=%async_computation.4 | async-start | bytes 294912 | tf_op jit(solution)/shard_map/reduce_scatter | solution.py:99
  674.7 5.6 copy-start
  674.7 5.6 copy-start.3
  677.0 169.3 %copy-start.1 = (bf16[2048,512]{1,0:T(8,128)(2,1)S(1)}, bf16[2048,512]{1,0:T(8,128)(2,1)}, u32[]{:S(2)}) copy-start(bf16[2048,512]{1,0:T(8,128)(2,1)} %all-gather.3.cloned.1.call-done) | copy-start | bytes 6291460
Sparse Core Ops, SparseCore 0:
  12.5 143.7 all-gather.2
  407.2 189.0 all-gather.4
  600.8 73.8 all-reduce.4
  848.7 91.4 reduce-scatter.1
